TPU v7x, 32 devices: a whole 2x2x4 slice. The times are simulated.
32 devices in a mesh: shard: 4 (over z), ctx: 4 (over y, core), tp: 2 (over x).
Axes of the slice: x: 2, y: 2, z: 4, core: 2. Of those that a mesh axis runs over, the one named last changes fastest.
Arguments:
- block_input: float32 [2048, 640], P(('shard', 'ctx')), may hold values from -6 to 6
- out_cotangent: float32 [2048, 640], P(('shard', 'ctx')), may hold values from -6 to 6
- seq_lengths: int32 [4, 4], P('shard'), may hold values from 1 to 256, 512 in all within a row
- q_weight: bfloat16 [640, 1024], P('shard', 'tp'), may hold values from -0.25 to 0.25
- k_weight: bfloat16 [640, 256], P('shard'), may hold values from -0.25 to 0.25
- v_weight: bfloat16 [640, 256], P('shard'), may hold values from -0.25 to 0.25
- o_weight: bfloat16 [640, 1024], P('shard', 'tp'), may hold values from -0.1875 to 0.1875
- gate_weight: bfloat16 [640, 2048], P('shard', 'tp'), may hold values from -0.25 to 0.25
- up_weight: bfloat16 [640, 2048], P('shard', 'tp'), may hold values from -0.25 to 0.25
- down_weight: bfloat16 [640, 2048], P('shard', 'tp'), may hold values from -0.125 to 0.125
- attn_in_gain: bfloat16 [640], P('shard'), may hold values from 0.25 to 1.75
- attn_out_gain: bfloat16 [640], P('shard'), may hold values from 0.25 to 1.75
- ffn_in_gain: bfloat16 [640], P('shard'), may hold values from 0.25 to 1.75
- ffn_out_gain: bfloat16 [640], P('shard'), may hold values from 0.25 to 1.75
- query_gain: bfloat16 [256], P('shard'), may hold values from 0.25 to 1.75
- key_gain: bfloat16 [256], P('shard'), may hold values from 0.25 to 1.75
Outputs:
- block_output: float32 [2048, 640], P(('shard', 'ctx'))
- input_grad: float32 [2048, 640], P(('shard', 'ctx'))
- q_weight_grad: float32 [640, 1024], P('shard', 'tp')
- k_weight_grad: float32 [640, 256], P('shard')
- v_weight_grad: float32 [640, 256], P('shard')
- o_weight_grad: float32 [640, 1024], P('shard', 'tp')
- gate_weight_grad: float32 [640, 2048], P('shard', 'tp')
- up_weight_grad: float32 [640, 2048], P('shard', 'tp')
- down_weight_grad: float32 [640, 2048], P('shard', 'tp')
- attn_in_gain_grad: float32 [640], P('shard')
- attn_out_gain_grad: float32 [640], P('shard')
- ffn_in_gain_grad: float32 [640], P('shard')
- ffn_out_gain_grad: float32 [640], P('shard')
- query_gain_grad: float32 [256], P('shard')
- key_gain_grad: float32 [256], P('shard')
Inputs may be any that keep to these rules, and one draw needn't show every extreme that they name: Row b of seq_lengths lists the 4 sequences packed into row b in order; they sum to 512, and the longest of every row has exactly 256 tokens.
All inputs are finite; a program needn't handle non-finite values.
Results may differ from a plain program's by a relative error of at most 0.015.
Values may be sent and summed in bfloat16 or wider, within the bound.
A program may use at most 64 MiB of HBM per device.

v0:
```python
import jax
import jax.numpy as jnp
from jax import lax
from jax.sharding import PartitionSpec as P

HD = 256
eps = 1e-06
rope_base = 1000000.0


def dot_plain(left, right):
    return jnp.dot(left, right, preferred_element_type=jnp.float32)


def dot_last(left, right):
    return lax.dot_general(
        left, right, (((1,), (1,)), ((), ())), preferred_element_type=jnp.float32
    )


def dot_first(left, right):
    return lax.dot_general(
        left, right, (((0,), (0,)), ((), ())), preferred_element_type=jnp.float32
    )


def norm_parts(value):
    scale = lax.rsqrt(jnp.mean(value * value, axis=-1, keepdims=True) + eps)
    return (value * scale, scale)


def norm_back(dnormed, unit, scale):
    return scale * (dnormed - unit * jnp.mean(dnormed * unit, axis=-1, keepdims=True))


def rope_tables(position):
    freq = rope_base ** (-jnp.arange(HD // 2).astype(jnp.float32) * (2.0 / HD))
    angle = position.astype(jnp.float32)[:, None] * freq[None, :]
    return (jnp.cos(angle), jnp.sin(angle))


def rotate(value, cosine, sine):
    half = value.shape[-1] // 2
    first, second = (value[..., :half], value[..., half:])
    return jnp.concatenate(
        [first * cosine - second * sine, second * cosine + first * sine], axis=-1
    )


def unrotate(value, cosine, sine):
    half = value.shape[-1] // 2
    first, second = (value[..., :half], value[..., half:])
    return jnp.concatenate(
        [first * cosine + second * sine, second * cosine - first * sine], axis=-1
    )


def layout(lengths, count):
    index = jnp.arange(count)
    ends = jnp.cumsum(lengths)
    after = (index[:, None] >= ends[None, :]).astype(jnp.int32)
    segment = jnp.sum(after, axis=1)
    position = index - jnp.sum(after * lengths[None, :], axis=1)
    return (segment, position)


def gelu_tanh(value):
    return jax.nn.gelu(value, approximate=True)


def masked_scores(query_head, key_block, mask, scaling):
    raw = dot_last(query_head, key_block) * scaling
    return jnp.where(mask, raw, -1e30)


def per_device(
    block_input,
    out_cotangent,
    seq_lengths,
    q_weight,
    k_weight,
    v_weight,
    o_weight,
    gate_weight,
    up_weight,
    down_weight,
    attn_in_gain,
    attn_out_gain,
    ffn_in_gain,
    ffn_out_gain,
    query_gain,
    key_gain,
):
    tokens = block_input.shape[0]
    width = block_input.shape[1]
    n_ctx = lax.axis_size("ctx")
    n_tp = lax.axis_size("tp")
    row_len = tokens * n_ctx
    piece = tokens // n_tp
    my_start = lax.axis_index("ctx") * tokens
    my_sub = lax.axis_index("tp") * piece
    scaling = HD ** (-0.5)
    segment, position = layout(seq_lengths[0], row_len)
    key_index = jnp.arange(row_len)
    query_index = my_start + jnp.arange(tokens)
    query_seg = lax.dynamic_slice_in_dim(segment, my_start, tokens)
    allowed = (query_seg[:, None] == segment[None, :]) & (
        key_index[None, :] <= query_index[:, None]
    )
    cosine, sine = rope_tables(lax.dynamic_slice_in_dim(position, my_start, tokens))
    gathered = (
        lax.all_gather(q_weight, "shard", axis=0, tiled=True),
        lax.all_gather(k_weight, "shard", axis=0, tiled=True),
        lax.all_gather(v_weight, "shard", axis=0, tiled=True),
        lax.all_gather(o_weight, "shard", axis=0, tiled=True),
        lax.all_gather(gate_weight, "shard", axis=0, tiled=True),
        lax.all_gather(up_weight, "shard", axis=0, tiled=True),
        lax.all_gather(down_weight, "shard", axis=0, tiled=True),
        lax.all_gather(attn_in_gain, "shard", axis=0, tiled=True),
        lax.all_gather(attn_out_gain, "shard", axis=0, tiled=True),
        lax.all_gather(ffn_in_gain, "shard", axis=0, tiled=True),
        lax.all_gather(ffn_out_gain, "shard", axis=0, tiled=True),
        lax.all_gather(query_gain, "shard", axis=0, tiled=True),
        lax.all_gather(key_gain, "shard", axis=0, tiled=True),
    )
    qw, kw, vw, ow, gw, uw, dw = gathered[:7]
    g_ai, g_ao, g_fi, g_fo, g_q, g_k = [item.astype(jnp.float32) for item in gathered[7:]]
    local_heads = qw.shape[1] // HD
    unit1, r1 = norm_parts(block_input)
    xn1 = (unit1 * g_ai).astype(jnp.bfloat16)
    qp = dot_plain(xn1, qw).reshape(tokens, local_heads, HD)
    qunit, rq = norm_parts(qp)
    queries = rotate(qunit * g_q, cosine[:, None, :], sine[:, None, :]).astype(jnp.bfloat16)
    kp = dot_plain(xn1, kw)
    kunit, rk = norm_parts(kp)
    keys = rotate(kunit * g_k, cosine, sine).astype(jnp.bfloat16)
    values = dot_plain(xn1, vw).astype(jnp.bfloat16)
    row_keys, row_values = (
        lax.all_gather(keys, "ctx", axis=0, tiled=True),
        lax.all_gather(values, "ctx", axis=0, tiled=True),
    )
    head_outs = []
    lses = []
    for head in range(local_heads):
        logits = masked_scores(queries[:, head, :], row_keys, allowed, scaling)
        peak = jnp.max(logits, axis=1, keepdims=True)
        lse = peak + jnp.log(jnp.sum(jnp.exp(logits - peak), axis=1, keepdims=True))
        weights = jnp.exp(logits - lse).astype(jnp.bfloat16)
        head_outs.append(dot_plain(weights, row_values))
        lses.append(lse)
    attended = jnp.concatenate(head_outs, axis=1).astype(jnp.bfloat16)
    proj = lax.psum(dot_last(attended, ow), "tp")
    aunit, ra = norm_parts(proj)
    h1 = block_input + aunit * g_ao
    unit2, r2 = norm_parts(h1)
    xn2 = (unit2 * g_fi).astype(jnp.bfloat16)
    gate = dot_plain(xn2, gw)
    up = dot_plain(xn2, uw)
    act, gelu_back = jax.vjp(gelu_tanh, gate)
    hidden = (act * up).astype(jnp.bfloat16)
    ffn = lax.psum(dot_last(hidden, dw), "tp")
    funit, rf = norm_parts(ffn)
    block_output = h1 + funit * g_fo
    back_keys, back_values = (row_keys, row_values)
    dg_fo = jnp.sum(out_cotangent * funit, axis=0)
    dffn = norm_back(out_cotangent * g_fo, funit, rf).astype(jnp.bfloat16)
    dhid = dot_plain(dffn, dw)
    d_down = dot_first(dffn, hidden)
    dup = (dhid * act).astype(jnp.bfloat16)
    dgate = gelu_back(dhid * up)[0].astype(jnp.bfloat16)
    d_gate_w = dot_first(xn2, dgate)
    d_up_w = dot_first(xn2, dup)
    dxn2 = lax.psum(dot_last(dgate, gw) + dot_last(dup, uw), "tp")
    dg_fi = jnp.sum(dxn2 * unit2, axis=0)
    dh1 = out_cotangent + norm_back(dxn2 * g_fi, unit2, r2)
    dg_ao = jnp.sum(dh1 * aunit, axis=0)
    dproj = norm_back(dh1 * g_ao, aunit, ra).astype(jnp.bfloat16)
    d_o_w = dot_first(dproj, attended)
    dattended = dot_plain(dproj, ow).astype(jnp.bfloat16)
    win_keys, win_values, win_allowed = (back_keys, back_values, allowed)
    key_terms = jnp.zeros((row_len, HD), jnp.float32)
    value_terms = jnp.zeros((row_len, HD), jnp.float32)
    dq_parts = []
    for head in range(local_heads):
        query_head = queries[:, head, :]
        out_head = attended[:, head * HD : (head + 1) * HD]
        dout_head = dattended[:, head * HD : (head + 1) * HD]
        logits = masked_scores(query_head, win_keys, win_allowed, scaling)
        weights = jnp.exp(logits - lses[head])
        weights_low = weights.astype(jnp.bfloat16)
        delta = jnp.sum(
            dout_head.astype(jnp.float32) * out_head.astype(jnp.float32), axis=1, keepdims=True
        )
        dprob = dot_last(dout_head, win_values)
        dscore = (weights * (dprob - delta) * scaling).astype(jnp.bfloat16)
        dq_parts.append(dot_plain(dscore, win_keys))
        key_terms = key_terms + dot_first(dscore, query_head)
        value_terms = value_terms + dot_first(weights_low, dout_head)
    dq = jnp.stack(dq_parts, axis=1)
    dqn = unrotate(dq, cosine[:, None, :], sine[:, None, :])
    dg_q = jnp.sum(dqn * qunit, axis=(0, 1))
    dqp = norm_back(dqn * g_q, qunit, rq).reshape(tokens, local_heads * HD).astype(jnp.bfloat16)
    dkeys, dvalues = (
        lax.psum_scatter(key_terms, ("ctx", "tp"), scatter_dimension=0, tiled=True),
        lax.psum_scatter(value_terms, ("ctx", "tp"), scatter_dimension=0, tiled=True),
    )
    kunit_rows = lax.dynamic_slice_in_dim(kunit, my_sub, piece, 0)
    rk_rows = lax.dynamic_slice_in_dim(rk, my_sub, piece, 0)
    cos_rows = lax.dynamic_slice_in_dim(cosine, my_sub, piece, 0)
    sin_rows = lax.dynamic_slice_in_dim(sine, my_sub, piece, 0)
    xn1_rows = lax.dynamic_slice_in_dim(xn1, my_sub, piece, 0)
    dkn = unrotate(dkeys, cos_rows, sin_rows)
    dg_k = jnp.sum(dkn * kunit_rows, axis=0)
    dkp = norm_back(dkn * g_k, kunit_rows, rk_rows).astype(jnp.bfloat16)
    dvr = dvalues.astype(jnp.bfloat16)
    shared_part = dot_last(dkp, kw) + dot_last(dvr, vw)
    placed = lax.dynamic_update_slice(
        jnp.zeros((tokens, width), jnp.float32), shared_part, (my_sub, jnp.zeros((), jnp.int32))
    )
    dxn1 = lax.psum(dot_last(dqp, qw) + placed, "tp")
    d_q_w = dot_first(xn1, dqp)
    d_k_w = dot_first(xn1_rows, dkp)
    d_v_w = dot_first(xn1_rows, dvr)
    dg_ai = jnp.sum(dxn1 * unit1, axis=0)
    input_grad = dh1 + norm_back(dxn1 * g_ai, unit1, r1)
    rows = (
        lax.psum_scatter(d_q_w, "shard", scatter_dimension=0, tiled=True),
        lax.psum_scatter(d_k_w, "shard", scatter_dimension=0, tiled=True),
        lax.psum_scatter(d_v_w, "shard", scatter_dimension=0, tiled=True),
        lax.psum_scatter(d_o_w, "shard", scatter_dimension=0, tiled=True),
        lax.psum_scatter(d_gate_w, "shard", scatter_dimension=0, tiled=True),
        lax.psum_scatter(d_up_w, "shard", scatter_dimension=0, tiled=True),
        lax.psum_scatter(d_down, "shard", scatter_dimension=0, tiled=True),
        lax.psum_scatter(dg_ai, "shard", scatter_dimension=0, tiled=True),
        lax.psum_scatter(dg_ao, "shard", scatter_dimension=0, tiled=True),
        lax.psum_scatter(dg_fi, "shard", scatter_dimension=0, tiled=True),
        lax.psum_scatter(dg_fo, "shard", scatter_dimension=0, tiled=True),
        lax.psum_scatter(dg_q, "shard", scatter_dimension=0, tiled=True),
        lax.psum_scatter(dg_k, "shard", scatter_dimension=0, tiled=True),
    )
    split_sums = lax.psum(
        (rows[0], rows[3], rows[4], rows[5], rows[6], rows[7], rows[8], rows[9], rows[10]), "ctx"
    )
    shared_sums = lax.psum((rows[1], rows[2], rows[11], rows[12]), ("ctx", "tp"))
    return (
        block_output,
        input_grad,
        split_sums[0],
        shared_sums[0],
        shared_sums[1],
        split_sums[1],
        split_sums[2],
        split_sums[3],
        split_sums[4],
        split_sums[5],
        split_sums[6],
        split_sums[7],
        split_sums[8],
        shared_sums[2],
        shared_sums[3],
    )


def solution(mesh):
    placed = (
        P(("shard", "ctx"), None),
        P(("shard", "ctx"), None),
        P("shard", None),
        P("shard", "tp"),
        P("shard", None),
        P("shard", None),
        P("shard", "tp"),
        P("shard", "tp"),
        P("shard", "tp"),
        P("shard", "tp"),
        P("shard"),
        P("shard"),
        P("shard"),
        P("shard"),
        P("shard"),
        P("shard"),
    )
    return jax.shard_map(
        per_device,
        mesh=mesh,
        in_specs=placed,
        out_specs=(
            P(("shard", "ctx"), None),
            P(("shard", "ctx"), None),
            P("shard", "tp"),
            P("shard", None),
            P("shard", None),
            P("shard", "tp"),
            P("shard", "tp"),
            P("shard", "tp"),
            P("shard", "tp"),
            P("shard"),
            P("shard"),
            P("shard"),
            P("shard"),
            P("shard"),
            P("shard"),
        ),
        check_vma=False,
    )
```

profile of v0, /device:TPU:0, one launch (start us, length us, event | category | flops | bytes accessed | tf_op | source)
XLA Modules:
  0.0 787.6 jit_solution(877558683739222252)
XLA Ops:
  8.1 1.3 fusion.54
  15.8 13.9 %all-reduce.17 = (bf16[640]{0:T(1024)(128)(2,1)S(1)}, bf16[256]{0:T(256)(128)(2,1)S(1)}, bf16[256]{0:T(256)(128)(2,1)S(1)}, bf16[640]{0:T(1024)(128)(2,1)S(1)}, ...) all-reduce(bf16[640]{0:T(1024)(128)(2,1)S(1)} %dynamic-update-slice, ...), channel_id=1, replica_groups=mesh['shard'=4,'ctx'=4,'tp'=2] {'shard'}, use_global_device_ids=true, to_apply=%add | all-reduce | flops 3072 | bytes 12288
  32.4 14.4 %all_gather.48 = bf16[640,256]{1,0:T(8,128)(2,1)S(1)} all-gather(bf16[160,256]{1,0:T(8,128)(2,1)} %param.20), channel_id=1, replica_groups=mesh['shard'=4,'ctx'=4,'tp'=2] {'shard'}, dimensions={0}, use_global_device_ids=true | all-gather | bytes 409600 | tf_op jit(solution)/shard_map/all_gather | solution.py:113
  46.8 1.2 multiply_convert_fusion.5
  49.5 5.8 all_gather.50
  55.3 17.0 %all_gather.46 = bf16[640,512]{1,0:T(8,128)(2,1)S(1)} all-gather(bf16[160,512]{1,0:T(8,128)(2,1)S(1)} %copy-done.46), channel_id=1, replica_groups=mesh['shard'=4,'ctx'=4,'tp'=2] {'shard'}, dimensions={0}, use_global_device_ids=true | all-gather | bytes 819200 | tf_op jit(solution)/shard_map/all_gather | solution.py:112
  74.1 16.6 %all_gather.53 = bf16[640,512]{1,0:T(8,128)(2,1)S(1)} all-gather(bf16[160,512]{1,0:T(8,128)(2,1)S(1)} %copy-done.47), channel_id=1, replica_groups=mesh['shard'=4,'ctx'=4,'tp'=2] {'shard'}, dimensions={0}, use_global_device_ids=true | all-gather | bytes 819200 | tf_op jit(solution)/shard_map/all_gather | solution.py:115
  90.7 14.7 %all_gather.51 = bf16[640,256]{1,0:T(8,128)(2,1)S(1)} all-gather(bf16[160,256]{1,0:T(8,128)(2,1)S(1)} %copy-done.48), channel_id=1, replica_groups=mesh['shard'=4,'ctx'=4,'tp'=2] {'shard'}, dimensions={0}, use_global_device_ids=true | all-gather | bytes 409600 | tf_op jit(solution)/shard_map/all_gather | solution.py:114
  105.6 5.8 all_gather.52
  116.3 22.7 %all-reduce.25.cloned.1.call-done = f32[128,640]{1,0:T(8,128)} async-done(((f32[128,640]{1,0:T(8,128)}), f32[128,640]{1,0:T(8,128)}) %all-reduce.25.cloned.1.call-update) | async-done | bytes 327696 | tf_op jit(solution)/shard_map/psum | solution.py:152
  141.4 7.5 all-gather.4.cloned.1.call-done
  148.8 2.5 fusion.58
  151.3 30.5 %all-gather.6.cloned.1.call-done = bf16[640,1024]{1,0:T(8,128)(2,1)} async-done(((bf16[160,1024]{1,0:T(8,128)(2,1)}), bf16[640,1024]{1,0:T(8,128)(2,1)}) %all-gather.6.cloned.1.call-update) | async-done | bytes 1310736 | tf_op jit(solution)/shard_map/all_gather | solution.py:117
  181.8 2.7 multiply_convert_fusion.1
  184.5 30.3 %all-gather.8.cloned.1.call-done = bf16[640,1024]{1,0:T(8,128)(2,1)} async-done(((bf16[160,1024]{1,0:T(8,128)(2,1)}), bf16[640,1024]{1,0:T(8,128)(2,1)}) %all-gather.8.cloned.1.call-update) | async-done | bytes 1310736 | tf_op jit(solution)/shard_map/all_gather | solution.py:118
  214.8 2.7 fusion.59
  217.5 23.6 %all-reduce.27.cloned.1.call-done = f32[128,640]{1,0:T(8,128)} async-done(((f32[128,640]{1,0:T(8,128)}), f32[128,640]{1,0:T(8,128)}) %all-reduce.27.cloned.1.call-update) | async-done | bytes 327696 | tf_op jit(solution)/shard_map/psum | solution.py:161
  241.2 1.2 multiply_reduce_fusion.8
  242.4 1.2 multiply_reduce_fusion
  243.6 1.8 multiply_convert_fusion.3
  247.8 1.3 convolution_add_fusion.2
  249.1 24.5 %all-reduce.29.cloned.1.call-done = f32[128,640]{1,0:T(8,128)} async-done(((f32[128,640]{1,0:T(8,128)}), f32[128,640]{1,0:T(8,128)}) %all-reduce.29.cloned.1.call-update) | async-done | bytes 327696 | tf_op jit(solution)/shard_map/psum | solution.py:173
  274.8 1.4 multiply_reduce_fusion.2
  280.3 32.6 %reduce-scatter.10.cloned.1.call-done = f32[64,256]{1,0:T(8,128)} async-done(((f32[512,256]{1,0:T(8,128)}), f32[64,256]{1,0:T(8,128)}) %reduce-scatter.10.cloned.1.call-update) | async-done | bytes 65552 | tf_op jit(solution)/shard_map/reduce_scatter | solution.py:204
  315.7 34.8 %reduce-scatter.12.cloned.1.call-done = f32[64,256]{1,0:T(8,128)} async-done(((f32[512,256]{1,0:T(8,128)}), f32[64,256]{1,0:T(8,128)}) %reduce-scatter.12.cloned.1.call-update) | async-done | bytes 65552 | tf_op jit(solution)/shard_map/reduce_scatter | solution.py:205
  350.5 2.0 fusion.25
  353.5 1.5 fusion.63
  355.3 1.4 fusion.23
  356.9 2.0 fusion.64
  359.8 2.1 fusion.65
  362.9 2.0 fusion.66
  367.2 8.7 %reduce-scatter.16.cloned.1.call-done = f32[160,256]{1,0:T(8,128)} async-done(((f32[640,256]{1,0:T(8,128)}), f32[160,256]{1,0:T(8,128)}) %reduce-scatter.16.cloned.1.call-update) | async-done | bytes 163856 | tf_op jit(solution)/shard_map/reduce_scatter | solution.py:228
  375.8 24.1 %reduce-scatter.18.cloned.1.call-done = f32[160,256]{1,0:T(8,128)} async-done(((f32[640,256]{1,0:T(8,128)}), f32[160,256]{1,0:T(8,128)}) %reduce-scatter.18.cloned.1.call-update) | async-done | bytes 163856 | tf_op jit(solution)/shard_map/reduce_scatter | solution.py:229
  400.1 32.3 %reduce-scatter.14.cloned.1.call-done = f32[160,512]{1,0:T(8,128)} async-done(((f32[640,512]{1,0:T(8,128)}), f32[160,512]{1,0:T(8,128)}) %reduce-scatter.14.cloned.1.call-update) | async-done | bytes 327696 | tf_op jit(solution)/shard_map/reduce_scatter | solution.py:227
  432.3 32.4 %reduce-scatter.20.cloned.1.call-done = f32[160,512]{1,0:T(8,128)} async-done(((f32[640,512]{1,0:T(8,128)}), f32[160,512]{1,0:T(8,128)}) %reduce-scatter.20.cloned.1.call-update) | async-done | bytes 327696 | tf_op jit(solution)/shard_map/reduce_scatter | solution.py:230
  464.7 53.1 %reduce-scatter.22.cloned.1.call-done = f32[160,1024]{1,0:T(8,128)} async-done(((f32[640,1024]{1,0:T(8,128)}), f32[160,1024]{1,0:T(8,128)}) %reduce-scatter.22.cloned.1.call-update) | async-done | bytes 655376 | tf_op jit(solution)/shard_map/reduce_scatter | solution.py:231
  517.8 54.1 %reduce-scatter.24.cloned.1.call-done = f32[160,1024]{1,0:T(8,128)} async-done(((f32[640,1024]{1,0:T(8,128)}), f32[160,1024]{1,0:T(8,128)}) %reduce-scatter.24.cloned.1.call-update) | async-done | bytes 655376 | tf_op jit(solution)/shard_map/reduce_scatter | solution.py:232
  572.0 54.0 %reduce-scatter.26.cloned.1.call-done = f32[160,1024]{1,0:T(8,128)} async-done(((f32[640,1024]{1,0:T(8,128)}), f32[160,1024]{1,0:T(8,128)}) %reduce-scatter.26.cloned.1.call-update) | async-done | bytes 655376 | tf_op jit(solution)/shard_map/reduce_scatter | solution.py:233
  627.4 25.4 %all-reduce.31.cloned.1.call-done = f32[128,640]{1,0:T(8,128)} async-done(((f32[128,640]{1,0:T(8,128)}), f32[128,640]{1,0:T(8,128)}) %all-reduce.31.cloned.1.call-update) | async-done | bytes 327696 | tf_op jit(solution)/shard_map/psum | solution.py:220
  654.0 19.0 %all-reduce.16 = (f32[640]{0:T(1024)S(1)}, f32[640]{0:T(1024)S(1)}, f32[640]{0:T(1024)S(1)}, f32[640]{0:T(1024)S(1)}, f32[256]{0:T(256)S(1)}, /*index=5*/f32[256]{0:T(256)S(1)}) all-reduce(f32[640]{0:T(1024)S(1)} %get-tuple-element.21, f32[640]{0:T(1024)S(1)} %get-tuple-element.19, ...), channel_id=11, replica_groups=mesh['shard'=4,'ctx'=4,'tp'=2] {'shard'}, use_global_device_ids=true, to_apply=%region_42.43.clone | all-reduce | flops 3072 | bytes 24576
  673.4 13.0 %all-reduce.12 = (f32[64]{0:T(128)}, f32[64]{0:T(128)}) all-reduce(f32[64]{0:T(128)S(1)} %dynamic-slice.20, f32[64]{0:T(128)S(1)} %dynamic-slice.22), channel_id=1, replica_groups=mesh['shard'=4,'ctx'=4,'tp'=2] {'ctx','tp'}, use_global_device_ids=true, to_apply=%region_56.57 | all-reduce | flops 128 | bytes 1024 | tf_op jit(solution)/shard_map/psum | solution.py:244
  686.3 7.6 all-reduce.14
  694.0 1.8 multiply_add_fusion
  695.8 14.3 %all-reduce.33.cloned.1.call-done = (f32[160,256]{1,0:T(8,128)}, f32[160,256]{1,0:T(8,128)}) async-done(((f32[160,256]{1,0:T(8,128)}, f32[160,256]{1,0:T(8,128)}), (f32[160,256]{1,0:T(8,128)}, f32[160,256]{1,0:T(8,128)})) %all-reduce.33.cloned.1.call-update) | async-done | bytes 327696 | tf_op jit(solution)/shard_map/psum | solution.py:244
  710.1 61.9 %all-reduce.35.cloned.1.call-done = (f32[160,512]{1,0:T(8,128)}, f32[160,512]{1,0:T(8,128)}, f32[160,1024]{1,0:T(8,128)}, f32[160,1024]{1,0:T(8,128)}, f32[160,1024]{1,0:T(8,128)}) async-done(((f32[160,512]{1,0:T(8,128)}, f32[160,512]{1,0:T(8,128)}, f32[160,1024]{1,0:T(8,128)}, f32[160,1024]{1,0:T(8,128)}, f32[160,1024]{1,0:T(8,128)}), (f32[160,512]{1,0:T(8,128)}, f32[160,512]{1,0:T(8,128)}, ...) | async-done | bytes 2621456 | tf_op jit(solution)/shard_map/psum | solution.py:241
  772.0 1.8 copy.85
  773.8 1.7 copy.86
  775.5 1.6 copy.87
  (254 shorter events, 38.8 us)
Async XLA Ops:
  8.0 130.9 %all-reduce.25.cloned.1.call-start = ((), (), s32[]{:S(2)}) async-start(), calls=%async_computation.9 | async-start | bytes 655360 | tf_op jit(solution)/shard_map/psum | solution.py:152
  30.8 24.5 %copy-start.49 = (f32[128]{0:T(128)}, f32[128]{0:T(128)S(1)}, u32[]{:S(2)}) copy-start(f32[128]{0:T(128)S(1)} %add_rsqrt_fusion.5) | copy-start | bytes 1540
  32.4 22.9 %copy-start.46 = (bf16[160,512]{1,0:T(8,128)(2,1)S(1)}, bf16[160,512]{1,0:T(8,128)(2,1)}, u32[]{:S(2)}) copy-start(bf16[160,512]{1,0:T(8,128)(2,1)} %param.19) | copy-start | bytes 491524
  46.8 25.5 %copy-start.11 = (bf16[640,256]{1,0:T(8,128)(2,1)}, bf16[640,256]{1,0:T(8,128)(2,1)S(1)}, u32[]{:S(2)}) copy-start(bf16[640,256]{1,0:T(8,128)(2,1)S(1)} %all_gather.48) | copy-start | bytes 983044
  48.3 24.3 %copy-start.53 = (f32[128]{0:T(128)}, f32[128]{0:T(128)S(1)}, u32[]{:S(2)}) copy-start(f32[128]{0:T(128)S(1)} %add_rsqrt_fusion.4) | copy-start | bytes 1540
  49.5 23.8 %copy-start.29 = (f32[128,128]{1,0:T(8,128)}, f32[128,128]{1,0:T(8,128)S(1)}, u32[]{:S(2)}) copy-start(f32[128,128]{1,0:T(8,128)S(1)} %get-tuple-element.75) | copy-start | bytes 196612
  49.5 23.8 %copy-start.31 = (f32[128,128]{1,0:T(8,128)}, f32[128,128]{1,0:T(8,128)S(1)}, u32[]{:S(2)}) copy-start(f32[128,128]{1,0:T(8,128)S(1)} %get-tuple-element.76) | copy-start | bytes 196612
  55.3 18.4 %copy-start.13 = (bf16[512,256]{1,0:T(8,128)(2,1)}, bf16[512,256]{1,0:T(8,128)(2,1)S(1)}, u32[]{:S(2)}) copy-start(bf16[512,256]{1,0:T(8,128)(2,1)S(1)} %all_gather.50) | copy-start | bytes 786436
  73.4 32.0 %copy-start.40 = (bf16[128,2,128]{2,0,1:T(8,128)(2,1)}, bf16[128,2,128]{2,0,1:T(8,128)(2,1)S(1)}, u32[]{:S(2)}) copy-start(bf16[128,2,128]{2,0,1:T(8,128)(2,1)S(1)} %get-tuple-element.66) | copy-start | bytes 196612
  73.4 17.3 %copy-start.48 = (bf16[160,256]{1,0:T(8,128)(2,1)S(1)}, bf16[160,256]{1,0:T(8,128)(2,1)}, u32[]{:S(2)}) copy-start(bf16[160,256]{1,0:T(8,128)(2,1)} %param.21) | copy-start | bytes 245764
  105.4 6.7 copy-start.9
  111.8 2.6 copy-start.51
  113.3 26.7 %copy-start = (f32[128,640]{1,0:T(8,128)S(1)}, f32[128,640]{1,0:T(8,128)}, u32[]{:S(2)}) copy-start(f32[128,640]{1,0:T(8,128)} %param.16) | copy-start | bytes 983044
  114.4 34.4 %all-gather.4.cloned.1.call-start = ((), (), s32[]{:S(2)}) async-start(), calls=%async_computation.10 | async-start | bytes 1638400 | tf_op jit(solution)/shard_map/all_gather | solution.py:116
  115.0 66.8 %all-gather.6.cloned.1.call-start = ((), (), s32[]{:S(2)}) async-start(), calls=%async_computation.11 | async-start | bytes 1638400 | tf_op jit(solution)/shard_map/all_gather | solution.py:117
  115.6 99.1 %all-gather.8.cloned.1.call-start = ((), (), s32[]{:S(2)}) async-start(), calls=%async_computation.12 | async-start | bytes 1638400 | tf_op jit(solution)/shard_map/all_gather | solution.py:118
  116.2 125.0 %all-reduce.27.cloned.1.call-start = ((), (), s32[]{:S(2)}) async-start(), calls=%async_computation.13 | async-start | bytes 655360 | tf_op jit(solution)/shard_map/psum | solution.py:161
  141.3 43.2 %copy-start.4 = (bf16[128,640]{1,0:T(8,128)(2,1)}, bf16[128,640]{1,0:T(8,128)(2,1)S(1)}, u32[]{:S(2)}) copy-start(bf16[128,640]{1,0:T(8,128)(2,1)S(1)} %multiply_convert_fusion.4) | copy-start | bytes 491524
  214.8 27.7 %copy-start.6 = (f32[128,640]{1,0:T(8,128)S(1)}, f32[128,640]{1,0:T(8,128)}, u32[]{:S(2)}) copy-start(f32[128,640]{1,0:T(8,128)} %param.17) | copy-start | bytes 983044
  217.5 56.1 %all-reduce.29.cloned.1.call-start = ((), (), s32[]{:S(2)}) async-start(), calls=%async_computation.14 | async-start | bytes 655360 | tf_op jit(solution)/shard_map/psum | solution.py:173
  241.2 4.3 copy-start.16
  241.2 4.3 copy-start.18
  241.2 4.3 copy-start.43
  247.7 27.0 %copy-start.1 = (f32[128,640]{1,0:T(8,128)S(1)}, f32[128,640]{1,0:T(8,128)}, u32[]{:S(2)}) copy-start(f32[128,640]{1,0:T(8,128)} %all-reduce.25.cloned.1.call-done) | copy-start | bytes 983044
  249.1 63.8 %reduce-scatter.10.cloned.1.call-start = ((), (), s32[]{:S(2)}) async-start(), calls=%async_computation.15 | async-start | bytes 589824 | tf_op jit(solution)/shard_map/reduce_scatter | solution.py:204
  274.8 1.9 copy-start.22
  274.8 1.9 copy-start.25
  278.6 71.9 %reduce-scatter.12.cloned.1.call-start = ((), (), s32[]{:S(2)}) async-start(), calls=%async_computation.16 | async-start | bytes 589824 | tf_op jit(solution)/shard_map/reduce_scatter | solution.py:205
  278.8 34.1 %copy-start.30 = (f32[128,128]{1,0:T(8,128)S(1)}, f32[128,128]{1,0:T(8,128)}, u32[]{:S(2)}) copy-start(f32[128,128]{1,0:T(8,128)} %copy-done.29) | copy-start | bytes 196612
  278.8 34.1 %copy-start.32 = (f32[128,128]{1,0:T(8,128)S(1)}, f32[128,128]{1,0:T(8,128)}, u32[]{:S(2)}) copy-start(f32[128,128]{1,0:T(8,128)} %copy-done.31) | copy-start | bytes 196612
  278.8 34.9 %copy-start.42 = (f32[128,256]{1,0:T(8,128)S(1)}, f32[128,256]{1,0:T(8,128)}, u32[]{:S(2)}) copy-start(f32[128,256]{1,0:T(8,128)} %get-tuple-element.58) | copy-start | bytes 393220
  280.3 95.6 %reduce-scatter.16.cloned.1.call-start = ((), (), s32[]{:S(2)}) async-start(), calls=%async_computation.19 | async-start | bytes 819200 | tf_op jit(solution)/shard_map/reduce_scatter | solution.py:228
  315.1 84.9 %reduce-scatter.18.cloned.1.call-start = ((), (), s32[]{:S(2)}) async-start(), calls=%async_computation.20 | async-start | bytes 819200 | tf_op jit(solution)/shard_map/reduce_scatter | solution.py:229
  352.5 79.8 %reduce-scatter.14.cloned.1.call-start = ((), (), s32[]{:S(2)}) async-start(), calls=%async_computation.18 | async-start | bytes 1638400 | tf_op jit(solution)/shard_map/reduce_scatter | solution.py:227
  353.5 1.8 copy-start.23
  353.5 1.8 copy-start.26
  355.1 109.6 %reduce-scatter.20.cloned.1.call-start = ((), (), s32[]{:S(2)}) async-start(), calls=%async_computation.21 | async-start | bytes 1638400 | tf_op jit(solution)/shard_map/reduce_scatter | solution.py:230
  356.8 161.0 %reduce-scatter.22.cloned.1.call-start = ((), (), s32[]{:S(2)}) async-start(), calls=%async_computation.22 | async-start | bytes 3276800 | tf_op jit(solution)/shard_map/reduce_scatter | solution.py:231
  358.9 213.1 %reduce-scatter.24.cloned.1.call-start = ((), (), s32[]{:S(2)}) async-start(), calls=%async_computation.23 | async-start | bytes 3276800 | tf_op jit(solution)/shard_map/reduce_scatter | solution.py:232
  361.9 264.0 %reduce-scatter.26.cloned.1.call-start = ((), (), s32[]{:S(2)}) async-start(), calls=%async_computation.24 | async-start | bytes 3276800 | tf_op jit(solution)/shard_map/reduce_scatter | solution.py:233
  365.0 287.8 %all-reduce.31.cloned.1.call-start = ((), (), s32[]{:S(2)}) async-start(), calls=%async_computation.17 | async-start | bytes 655360 | tf_op jit(solution)/shard_map/psum | solution.py:220
  367.1 343.0 %all-reduce.33.cloned.1.call-start = ((), (), s32[]{:S(2)}) async-start(), calls=%async_computation.25 | async-start | bytes 655360 | tf_op jit(solution)/shard_map/psum | solution.py:244
  400.0 372.0 %all-reduce.35.cloned.1.call-start = ((), (), s32[]{:S(2)}) async-start(), calls=%async_computation.26 | async-start | bytes 5242880 | tf_op jit(solution)/shard_map/psum | solution.py:241
  626.0 26.8 %copy-start.50 = (f32[128]{0:T(128)S(1)}, f32[128]{0:T(128)}, u32[]{:S(2)}) copy-start(f32[128]{0:T(128)} %copy-done.49) | copy-start | bytes 1540
  626.0 68.0 %copy-start.8 = (f32[128,640]{1,0:T(8,128)S(1)}, f32[128,640]{1,0:T(8,128)}, u32[]{:S(2)}) copy-start(f32[128,640]{1,0:T(8,128)} %copy-done.7) | copy-start | bytes 983044
  772.0 5.1 copy-start.44
  772.0 5.8 copy-start.37
  773.8 4.8 copy-start.36
  (25 other events, 27.9 us)
Sparse Core Ops, SparseCore 0:
  114.5 24.3 all-reduce.24
  217.6 23.4 all-reduce.26
  249.2 24.3 all-reduce.28
  278.7 34.1 reduce-scatter.9
  316.4 34.0 reduce-scatter.11
  353.3 22.5 reduce-scatter.15
  378.7 21.2 reduce-scatter.17
  402.3 30.0 reduce-scatter.13
  434.6 30.0 reduce-scatter.19
  466.9 50.9 reduce-scatter.21
  520.1 51.7 reduce-scatter.23
  574.1 51.7 reduce-scatter.25
  628.8 23.8 all-reduce.30
  655.7 54.3 all-reduce.32
  712.6 59.3 all-reduce.34
Sparse Core Ops, SparseCore 1:
  116.5 32.3 all-gather.3
  150.3 31.5 all-gather.5
  183.2 31.5 all-gather.7
where the time goes:
time: 789 us; the launch traced here: 788 us
  waiting for transfers between devices  568 us (72%)
  blocking collectives  128 us (16%)
  matrix products  30.1 us (4%)
  local copies, waits for them, and re-layouts  21.5 us (3%)
  other arithmetic  19.7 us (2%)
  between operations  19.2 us (2%)
    psum x1, waiting for transfers between devices, per_device(): lax.psum((rows[0], rows[3], rows[4], rows[5], rows[6], rows[7], rows[8],...  61.9 us
    reduce_scatter x1, waiting for transfers between devices, per_device(): lax.psum_scatter(d_up_w, 'shard', scatter_dimension=0, tiled=True)  54.1 us
    reduce_scatter x1, waiting for transfers between devices, per_device(): lax.psum_scatter(d_down, 'shard', scatter_dimension=0, tiled=True)  54 us
    reduce_scatter x1, waiting for transfers between devices, per_device(): lax.psum_scatter(d_gate_w, 'shard', scatter_dimension=0, tiled=True)  53.1 us
    reduce_scatter x1, waiting for transfers between devices, per_device(): lax.psum_scatter(value_terms, ('ctx', 'tp'), scatter_dimension=0, tiled=T...  34.8 us
    unnamed x2, blocking collectives  32.9 us
    reduce_scatter x1, waiting for transfers between devices, per_device(): lax.psum_scatter(key_terms, ('ctx', 'tp'), scatter_dimension=0, tiled=True)  32.6 us
    reduce_scatter x1, waiting for transfers between devices, per_device(): lax.psum_scatter(d_o_w, 'shard', scatter_dimension=0, tiled=True)  32.4 us
  transfers between devices with their start and end apart: 18, of which 18 were waited for; matrix products, arithmetic and copies ran while one was open for 4% of the time, Pallas kernels for 0%

commit v1 on v0

--- a/solution.py
+++ b/solution.py
@@ -217,7 +217,7 @@
     placed = lax.dynamic_update_slice(
         jnp.zeros((tokens, width), jnp.float32), shared_part, (my_sub, jnp.zeros((), jnp.int32))
     )
-    dxn1 = lax.psum(dot_last(dqp, qw) + placed, "tp")
+    dxn1 = jnp.sum(lax.all_gather(dot_last(dqp, qw) + placed, "tp"), axis=0)
     d_q_w = dot_first(xn1, dqp)
     d_k_w = dot_first(xn1_rows, dkp)
     d_v_w = dot_first(xn1_rows, dvr)

time: 789 us -> 762 us (0.966)
  waiting for transfers between devices: 568 us -> 534 us
  blocking collectives: 128 us -> 137 us
    psum x1 -> x0, waiting for transfers between devices: 25.4 us -> none  [per_device(): dxn1 = lax.psum(dot_last(dqp, qw) + placed, 'tp')]
    all_gather x0 -> x1, blocking collectives: none -> 10.3 us  [per_device(): dxn1 = jnp.sum(lax.all_gather(dot_last(dqp, qw) + placed, 'tp'), axis=0)]
    psum x1, waiting for transfers between devices: 14.3 us -> 4.53 us  [per_device(): lax.psum((rows[1], rows[2], rows[11], rows[12]), ('ctx', 'tp'))]
    unnamed x141 -> x140, local copies, waits for them, and re-layouts: 20.6 us -> 19.9 us
  transfers between devices with their start and end apart: 18 -> 17, of which waited for: 18 -> 17; matrix products, arithmetic and copies ran while one was open for 4% -> 3% of each run, Pallas kernels for 0% -> 0%
where the time goes in v1:
time: 762 us; the launch traced here: 761 us
  waiting for transfers between devices  534 us (70%)
  blocking collectives  137 us (18%)
  matrix products  30.1 us (4%)
  local copies, waits for them, and re-layouts  20.8 us (3%)
  between operations  19.2 us (3%)
  other arithmetic  17.8 us (2%)
    psum x1, waiting for transfers between devices, per_device(): lax.psum((rows[0], rows[3], rows[4], rows[5], rows[6], rows[7], rows[8],...  61.9 us
    reduce_scatter x1, waiting for transfers between devices, per_device(): lax.psum_scatter(d_up_w, 'shard', scatter_dimension=0, tiled=True)  54.1 us
    reduce_scatter x1, waiting for transfers between devices, per_device(): lax.psum_scatter(d_down, 'shard', scatter_dimension=0, tiled=True)  54 us
    reduce_scatter x1, waiting for transfers between devices, per_device(): lax.psum_scatter(d_gate_w, 'shard', scatter_dimension=0, tiled=True)  53.1 us
    reduce_scatter x1, waiting for transfers between devices, per_device(): lax.psum_scatter(value_terms, ('ctx', 'tp'), scatter_dimension=0, tiled=T...  34.8 us
    reduce_scatter x1, waiting for transfers between devices, per_device(): lax.psum_scatter(key_terms, ('ctx', 'tp'), scatter_dimension=0, tiled=True)  32.6 us
    reduce_scatter x1, waiting for transfers between devices, per_device(): lax.psum_scatter(d_o_w, 'shard', scatter_dimension=0, tiled=True)  32.4 us
    unnamed x2, blocking collectives  31.4 us
  transfers between devices with their start and end apart: 17, of which 17 were waited for; matrix products, arithmetic and copies ran while one was open for 3% of the time, Pallas kernels for 0%

profile of v1, /device:TPU:0, one launch (start us, length us, event | category | flops | bytes accessed | tf_op | source)
XLA Modules:
  0.0 760.5 jit_solution(3166556825457189490)
XLA Ops:
  8.1 1.3 fusion.55
  15.8 13.9 %all-reduce.17 = (bf16[640]{0:T(1024)(128)(2,1)S(1)}, bf16[256]{0:T(256)(128)(2,1)S(1)}, bf16[256]{0:T(256)(128)(2,1)S(1)}, bf16[640]{0:T(1024)(128)(2,1)S(1)}, ...) all-reduce(bf16[640]{0:T(1024)(128)(2,1)S(1)} %dynamic-update-slice, ...), channel_id=1, replica_groups=mesh['shard'=4,'ctx'=4,'tp'=2] {'shard'}, use_global_device_ids=true, to_apply=%add | all-reduce | flops 3072 | bytes 12288
  32.4 14.4 %all_gather.56 = bf16[640,256]{1,0:T(8,128)(2,1)S(1)} all-gather(bf16[160,256]{1,0:T(8,128)(2,1)} %param.20), channel_id=1, replica_groups=mesh['shard'=4,'ctx'=4,'tp'=2] {'shard'}, dimensions={0}, use_global_device_ids=true | all-gather | bytes 409600 | tf_op jit(solution)/shard_map/all_gather | solution.py:113
  46.8 1.2 multiply_convert_fusion.5
  49.5 5.8 all_gather.58
  55.3 17.0 %all_gather.54 = bf16[640,512]{1,0:T(8,128)(2,1)S(1)} all-gather(bf16[160,512]{1,0:T(8,128)(2,1)S(1)} %copy-done.45), channel_id=1, replica_groups=mesh['shard'=4,'ctx'=4,'tp'=2] {'shard'}, dimensions={0}, use_global_device_ids=true | all-gather | bytes 819200 | tf_op jit(solution)/shard_map/all_gather | solution.py:112
  74.1 16.5 %all_gather.61 = bf16[640,512]{1,0:T(8,128)(2,1)S(1)} all-gather(bf16[160,512]{1,0:T(8,128)(2,1)S(1)} %copy-done.46), channel_id=1, replica_groups=mesh['shard'=4,'ctx'=4,'tp'=2] {'shard'}, dimensions={0}, use_global_device_ids=true | all-gather | bytes 819200 | tf_op jit(solution)/shard_map/all_gather | solution.py:115
  90.6 14.6 %all_gather.59 = bf16[640,256]{1,0:T(8,128)(2,1)S(1)} all-gather(bf16[160,256]{1,0:T(8,128)(2,1)S(1)} %copy-done.47), channel_id=1, replica_groups=mesh['shard'=4,'ctx'=4,'tp'=2] {'shard'}, dimensions={0}, use_global_device_ids=true | all-gather | bytes 409600 | tf_op jit(solution)/shard_map/all_gather | solution.py:114
  105.5 5.8 all_gather.60
  116.1 22.8 %all-reduce.24.cloned.1.call-done = f32[128,640]{1,0:T(8,128)} async-done(((f32[128,640]{1,0:T(8,128)}), f32[128,640]{1,0:T(8,128)}) %all-reduce.24.cloned.1.call-update) | async-done | bytes 327696 | tf_op jit(solution)/shard_map/psum | solution.py:152
  141.4 7.5 all-gather.4.cloned.1.call-done
  148.8 2.5 fusion.59
  151.3 30.5 %all-gather.6.cloned.1.call-done = bf16[640,1024]{1,0:T(8,128)(2,1)} async-done(((bf16[160,1024]{1,0:T(8,128)(2,1)}), bf16[640,1024]{1,0:T(8,128)(2,1)}) %all-gather.6.cloned.1.call-update) | async-done | bytes 1310736 | tf_op jit(solution)/shard_map/all_gather | solution.py:117
  181.8 2.7 multiply_convert_fusion.1
  184.5 30.3 %all-gather.8.cloned.1.call-done = bf16[640,1024]{1,0:T(8,128)(2,1)} async-done(((bf16[160,1024]{1,0:T(8,128)(2,1)}), bf16[640,1024]{1,0:T(8,128)(2,1)}) %all-gather.8.cloned.1.call-update) | async-done | bytes 1310736 | tf_op jit(solution)/shard_map/all_gather | solution.py:118
  214.8 2.7 fusion.60
  217.6 23.6 %all-reduce.26.cloned.1.call-done = f32[128,640]{1,0:T(8,128)} async-done(((f32[128,640]{1,0:T(8,128)}), f32[128,640]{1,0:T(8,128)}) %all-reduce.26.cloned.1.call-update) | async-done | bytes 327696 | tf_op jit(solution)/shard_map/psum | solution.py:161
  241.2 1.2 multiply_reduce_fusion.8
  242.4 1.2 multiply_reduce_fusion
  243.6 1.8 multiply_convert_fusion.3
  247.8 1.3 convolution_add_fusion.2
  249.1 24.5 %all-reduce.28.cloned.1.call-done = f32[128,640]{1,0:T(8,128)} async-done(((f32[128,640]{1,0:T(8,128)}), f32[128,640]{1,0:T(8,128)}) %all-reduce.28.cloned.1.call-update) | async-done | bytes 327696 | tf_op jit(solution)/shard_map/psum | solution.py:173
  273.6 1.2 multiply_reduce_fusion.1
  274.8 1.4 multiply_reduce_fusion.2
  280.3 32.6 %reduce-scatter.10.cloned.1.call-done = f32[64,256]{1,0:T(8,128)} async-done(((f32[512,256]{1,0:T(8,128)}), f32[64,256]{1,0:T(8,128)}) %reduce-scatter.10.cloned.1.call-update) | async-done | bytes 65552 | tf_op jit(solution)/shard_map/reduce_scatter | solution.py:204
  315.7 34.8 %reduce-scatter.12.cloned.1.call-done = f32[64,256]{1,0:T(8,128)} async-done(((f32[512,256]{1,0:T(8,128)}), f32[64,256]{1,0:T(8,128)}) %reduce-scatter.12.cloned.1.call-update) | async-done | bytes 65552 | tf_op jit(solution)/shard_map/reduce_scatter | solution.py:205
  350.6 2.0 fusion.26
  353.5 1.5 fusion.64
  355.3 1.4 fusion.24
  356.9 2.0 fusion.65
  359.8 2.1 fusion.66
  362.9 2.0 fusion.67
  365.0 10.9 %reduce-scatter.16.cloned.1.call-done = f32[160,256]{1,0:T(8,128)} async-done(((f32[640,256]{1,0:T(8,128)}), f32[160,256]{1,0:T(8,128)}) %reduce-scatter.16.cloned.1.call-update) | async-done | bytes 163856 | tf_op jit(solution)/shard_map/reduce_scatter | solution.py:228
  375.9 24.1 %reduce-scatter.18.cloned.1.call-done = f32[160,256]{1,0:T(8,128)} async-done(((f32[640,256]{1,0:T(8,128)}), f32[160,256]{1,0:T(8,128)}) %reduce-scatter.18.cloned.1.call-update) | async-done | bytes 163856 | tf_op jit(solution)/shard_map/reduce_scatter | solution.py:229
  401.4 31.0 %reduce-scatter.14.cloned.1.call-done = f32[160,512]{1,0:T(8,128)} async-done(((f32[640,512]{1,0:T(8,128)}), f32[160,512]{1,0:T(8,128)}) %reduce-scatter.14.cloned.1.call-update) | async-done | bytes 327696 | tf_op jit(solution)/shard_map/reduce_scatter | solution.py:227
  432.3 32.4 %reduce-scatter.20.cloned.1.call-done = f32[160,512]{1,0:T(8,128)} async-done(((f32[640,512]{1,0:T(8,128)}), f32[160,512]{1,0:T(8,128)}) %reduce-scatter.20.cloned.1.call-update) | async-done | bytes 327696 | tf_op jit(solution)/shard_map/reduce_scatter | solution.py:230
  464.7 53.1 %reduce-scatter.22.cloned.1.call-done = f32[160,1024]{1,0:T(8,128)} async-done(((f32[640,1024]{1,0:T(8,128)}), f32[160,1024]{1,0:T(8,128)}) %reduce-scatter.22.cloned.1.call-update) | async-done | bytes 655376 | tf_op jit(solution)/shard_map/reduce_scatter | solution.py:231
  517.8 54.1 %reduce-scatter.24.cloned.1.call-done = f32[160,1024]{1,0:T(8,128)} async-done(((f32[640,1024]{1,0:T(8,128)}), f32[160,1024]{1,0:T(8,128)}) %reduce-scatter.24.cloned.1.call-update) | async-done | bytes 655376 | tf_op jit(solution)/shard_map/reduce_scatter | solution.py:232
  572.0 54.0 %reduce-scatter.26.cloned.1.call-done = f32[160,1024]{1,0:T(8,128)} async-done(((f32[640,1024]{1,0:T(8,128)}), f32[160,1024]{1,0:T(8,128)}) %reduce-scatter.26.cloned.1.call-update) | async-done | bytes 655376 | tf_op jit(solution)/shard_map/reduce_scatter | solution.py:233
  627.5 10.3 %all_gather.70 = f32[2,128,640]{2,1,0:T(8,128)S(1)} all-gather(f32[1,128,640]{2,1,0:T(8,128)S(1)} %fusion.10), channel_id=1, replica_groups=mesh['shard'=4,'ctx'=4,'tp'=2] {'tp'}, dimensions={0}, use_global_device_ids=true | all-gather | bytes 983040 | tf_op jit(solution)/shard_map/all_gather | solution.py:220
  638.0 17.4 %all-reduce.16 = (f32[640]{0:T(1024)S(1)}, f32[640]{0:T(1024)S(1)}, f32[640]{0:T(1024)S(1)}, f32[640]{0:T(1024)S(1)}, f32[256]{0:T(256)S(1)}, /*index=5*/f32[256]{0:T(256)S(1)}) all-reduce(f32[640]{0:T(1024)S(1)} %get-tuple-element.21, f32[640]{0:T(1024)S(1)} %get-tuple-element.19, ...), channel_id=11, replica_groups=mesh['shard'=4,'ctx'=4,'tp'=2] {'shard'}, use_global_device_ids=true, to_apply=%region_42.43.clone | all-reduce | flops 3072 | bytes 24576
  655.9 14.2 %all-reduce.12 = (f32[64]{0:T(128)}, f32[64]{0:T(128)}) all-reduce(f32[64]{0:T(128)S(1)} %dynamic-slice.20, f32[64]{0:T(128)S(1)} %dynamic-slice.22), channel_id=1, replica_groups=mesh['shard'=4,'ctx'=4,'tp'=2] {'ctx','tp'}, use_global_device_ids=true, to_apply=%region_56.57 | all-reduce | flops 128 | bytes 1024 | tf_op jit(solution)/shard_map/psum | solution.py:244
  670.1 7.4 all-reduce.14
  678.4 4.5 all-reduce.30.cloned.1.call-done
  683.0 61.9 %all-reduce.32.cloned.1.call-done = (f32[160,512]{1,0:T(8,128)}, f32[160,512]{1,0:T(8,128)}, f32[160,1024]{1,0:T(8,128)}, f32[160,1024]{1,0:T(8,128)}, f32[160,1024]{1,0:T(8,128)}) async-done(((f32[160,512]{1,0:T(8,128)}, f32[160,512]{1,0:T(8,128)}, f32[160,1024]{1,0:T(8,128)}, f32[160,1024]{1,0:T(8,128)}, f32[160,1024]{1,0:T(8,128)}), (f32[160,512]{1,0:T(8,128)}, f32[160,512]{1,0:T(8,128)}, ...) | async-done | bytes 2621456 | tf_op jit(solution)/shard_map/psum | solution.py:241
  744.9 1.8 copy.84
  746.7 1.7 copy.85
  748.3 1.6 copy.86
  (252 shorter events, 36.8 us)
Async XLA Ops:
  8.0 130.9 %all-reduce.24.cloned.1.call-start = ((), (), s32[]{:S(2)}) async-start(), calls=%async_computation.9 | async-start | bytes 655360 | tf_op jit(solution)/shard_map/psum | solution.py:152
  30.8 24.5 %copy-start.48 = (f32[128]{0:T(128)}, f32[128]{0:T(128)S(1)}, u32[]{:S(2)}) copy-start(f32[128]{0:T(128)S(1)} %add_rsqrt_fusion.5) | copy-start | bytes 1540
  32.4 22.9 %copy-start.45 = (bf16[160,512]{1,0:T(8,128)(2,1)S(1)}, bf16[160,512]{1,0:T(8,128)(2,1)}, u32[]{:S(2)}) copy-start(bf16[160,512]{1,0:T(8,128)(2,1)} %param.19) | copy-start | bytes 491524
  46.8 2.7 copy-start.11
  48.3 24.3 %copy-start.52 = (f32[128]{0:T(128)}, f32[128]{0:T(128)S(1)}, u32[]{:S(2)}) copy-start(f32[128]{0:T(128)S(1)} %add_rsqrt_fusion.4) | copy-start | bytes 1540
  49.5 23.8 %copy-start.28 = (f32[128,128]{1,0:T(8,128)}, f32[128,128]{1,0:T(8,128)S(1)}, u32[]{:S(2)}) copy-start(f32[128,128]{1,0:T(8,128)S(1)} %get-tuple-element.75) | copy-start | bytes 196612
  49.5 23.8 %copy-start.30 = (f32[128,128]{1,0:T(8,128)}, f32[128,128]{1,0:T(8,128)S(1)}, u32[]{:S(2)}) copy-start(f32[128,128]{1,0:T(8,128)S(1)} %get-tuple-element.76) | copy-start | bytes 196612
  55.3 18.4 %copy-start.13 = (bf16[512,256]{1,0:T(8,128)(2,1)}, bf16[512,256]{1,0:T(8,128)(2,1)S(1)}, u32[]{:S(2)}) copy-start(bf16[512,256]{1,0:T(8,128)(2,1)S(1)} %all_gather.58) | copy-start | bytes 786436
  73.4 31.9 %copy-start.37 = (bf16[128,2,128]{2,0,1:T(8,128)(2,1)}, bf16[128,2,128]{2,0,1:T(8,128)(2,1)S(1)}, u32[]{:S(2)}) copy-start(bf16[128,2,128]{2,0,1:T(8,128)(2,1)S(1)} %get-tuple-element.65) | copy-start | bytes 196612
  73.4 31.9 %copy-start.39 = (bf16[128,2,128]{2,0,1:T(8,128)(2,1)}, bf16[128,2,128]{2,0,1:T(8,128)(2,1)S(1)}, u32[]{:S(2)}) copy-start(bf16[128,2,128]{2,0,1:T(8,128)(2,1)S(1)} %get-tuple-element.66) | copy-start | bytes 196612
  73.4 17.2 %copy-start.47 = (bf16[160,256]{1,0:T(8,128)(2,1)S(1)}, bf16[160,256]{1,0:T(8,128)(2,1)}, u32[]{:S(2)}) copy-start(bf16[160,256]{1,0:T(8,128)(2,1)} %param.21) | copy-start | bytes 245764
  105.3 6.7 copy-start.9
  111.7 2.6 copy-start.50
  113.2 26.8 %copy-start = (f32[128,640]{1,0:T(8,128)S(1)}, f32[128,640]{1,0:T(8,128)}, u32[]{:S(2)}) copy-start(f32[128,640]{1,0:T(8,128)} %param.16) | copy-start | bytes 983044
  114.3 34.5 %all-gather.4.cloned.1.call-start = ((), (), s32[]{:S(2)}) async-start(), calls=%async_computation.10 | async-start | bytes 1638400 | tf_op jit(solution)/shard_map/all_gather | solution.py:116
  114.9 66.9 %all-gather.6.cloned.1.call-start = ((), (), s32[]{:S(2)}) async-start(), calls=%async_computation.11 | async-start | bytes 1638400 | tf_op jit(solution)/shard_map/all_gather | solution.py:117
  115.5 99.3 %all-gather.8.cloned.1.call-start = ((), (), s32[]{:S(2)}) async-start(), calls=%async_computation.12 | async-start | bytes 1638400 | tf_op jit(solution)/shard_map/all_gather | solution.py:118
  116.1 125.1 %all-reduce.26.cloned.1.call-start = ((), (), s32[]{:S(2)}) async-start(), calls=%async_computation.13 | async-start | bytes 655360 | tf_op jit(solution)/shard_map/psum | solution.py:161
  141.3 43.2 %copy-start.4 = (bf16[128,640]{1,0:T(8,128)(2,1)}, bf16[128,640]{1,0:T(8,128)(2,1)S(1)}, u32[]{:S(2)}) copy-start(bf16[128,640]{1,0:T(8,128)(2,1)S(1)} %multiply_convert_fusion.4) | copy-start | bytes 491524
  214.8 27.7 %copy-start.6 = (f32[128,640]{1,0:T(8,128)S(1)}, f32[128,640]{1,0:T(8,128)}, u32[]{:S(2)}) copy-start(f32[128,640]{1,0:T(8,128)} %param.17) | copy-start | bytes 983044
  217.5 56.1 %all-reduce.28.cloned.1.call-start = ((), (), s32[]{:S(2)}) async-start(), calls=%async_computation.14 | async-start | bytes 655360 | tf_op jit(solution)/shard_map/psum | solution.py:173
  241.2 4.3 copy-start.16
  241.2 4.3 copy-start.17
  241.2 4.3 copy-start.42
  247.8 27.0 %copy-start.1 = (f32[128,640]{1,0:T(8,128)S(1)}, f32[128,640]{1,0:T(8,128)}, u32[]{:S(2)}) copy-start(f32[128,640]{1,0:T(8,128)} %all-reduce.24.cloned.1.call-done) | copy-start | bytes 983044
  249.1 63.8 %reduce-scatter.10.cloned.1.call-start = ((), (), s32[]{:S(2)}) async-start(), calls=%async_computation.15 | async-start | bytes 589824 | tf_op jit(solution)/shard_map/reduce_scatter | solution.py:204
  274.8 1.9 copy-start.21
  274.8 1.9 copy-start.24
  278.6 71.9 %reduce-scatter.12.cloned.1.call-start = ((), (), s32[]{:S(2)}) async-start(), calls=%async_computation.16 | async-start | bytes 589824 | tf_op jit(solution)/shard_map/reduce_scatter | solution.py:205
  278.8 34.1 %copy-start.29 = (f32[128,128]{1,0:T(8,128)S(1)}, f32[128,128]{1,0:T(8,128)}, u32[]{:S(2)}) copy-start(f32[128,128]{1,0:T(8,128)} %copy-done.28) | copy-start | bytes 196612
  278.8 34.1 %copy-start.31 = (f32[128,128]{1,0:T(8,128)S(1)}, f32[128,128]{1,0:T(8,128)}, u32[]{:S(2)}) copy-start(f32[128,128]{1,0:T(8,128)} %copy-done.30) | copy-start | bytes 196612
  278.8 34.9 %copy-start.41 = (f32[128,256]{1,0:T(8,128)S(1)}, f32[128,256]{1,0:T(8,128)}, u32[]{:S(2)}) copy-start(f32[128,256]{1,0:T(8,128)} %get-tuple-element.58) | copy-start | bytes 393220
  280.3 95.6 %reduce-scatter.16.cloned.1.call-start = ((), (), s32[]{:S(2)}) async-start(), calls=%async_computation.18 | async-start | bytes 819200 | tf_op jit(solution)/shard_map/reduce_scatter | solution.py:228
  315.1 84.9 %reduce-scatter.18.cloned.1.call-start = ((), (), s32[]{:S(2)}) async-start(), calls=%async_computation.19 | async-start | bytes 819200 | tf_op jit(solution)/shard_map/reduce_scatter | solution.py:229
  352.5 79.8 %reduce-scatter.14.cloned.1.call-start = ((), (), s32[]{:S(2)}) async-start(), calls=%async_computation.17 | async-start | bytes 1638400 | tf_op jit(solution)/shard_map/reduce_scatter | solution.py:227
  353.5 1.8 copy-start.22
  353.5 1.8 copy-start.25
  355.1 109.6 %reduce-scatter.20.cloned.1.call-start = ((), (), s32[]{:S(2)}) async-start(), calls=%async_computation.20 | async-start | bytes 1638400 | tf_op jit(solution)/shard_map/reduce_scatter | solution.py:230
  356.8 161.1 %reduce-scatter.22.cloned.1.call-start = ((), (), s32[]{:S(2)}) async-start(), calls=%async_computation.21 | async-start | bytes 3276800 | tf_op jit(solution)/shard_map/reduce_scatter | solution.py:231
  358.9 213.1 %reduce-scatter.24.cloned.1.call-start = ((), (), s32[]{:S(2)}) async-start(), calls=%async_computation.22 | async-start | bytes 3276800 | tf_op jit(solution)/shard_map/reduce_scatter | solution.py:232
  361.9 264.1 %reduce-scatter.26.cloned.1.call-start = ((), (), s32[]{:S(2)}) async-start(), calls=%async_computation.23 | async-start | bytes 3276800 | tf_op jit(solution)/shard_map/reduce_scatter | solution.py:233
  365.0 318.0 %all-reduce.30.cloned.1.call-start = ((), (), s32[]{:S(2)}) async-start(), calls=%async_computation.24 | async-start | bytes 655360 | tf_op jit(solution)/shard_map/psum | solution.py:244
  400.0 344.8 %all-reduce.32.cloned.1.call-start = ((), (), s32[]{:S(2)}) async-start(), calls=%async_computation.25 | async-start | bytes 5242880 | tf_op jit(solution)/shard_map/psum | solution.py:241
  627.2 10.6 %copy-start.49 = (f32[128]{0:T(128)S(1)}, f32[128]{0:T(128)}, u32[]{:S(2)}) copy-start(f32[128]{0:T(128)} %copy-done.48) | copy-start | bytes 1540
  627.5 50.1 %copy-start.8 = (f32[128,640]{1,0:T(8,128)S(1)}, f32[128,640]{1,0:T(8,128)}, u32[]{:S(2)}) copy-start(f32[128,640]{1,0:T(8,128)} %copy-done.7) | copy-start | bytes 983044
  744.9 5.1 copy-start.43
  744.9 5.8 copy-start.36
  746.7 4.8 copy-start.35
  (23 other events, 26.5 us)
Sparse Core Ops, SparseCore 0:
  114.4 24.4 all-reduce.23
  217.6 23.4 all-reduce.25
  249.2 24.3 all-reduce.27
  278.8 34.1 reduce-scatter.9
  316.4 34.0 reduce-scatter.11
  353.3 22.5 reduce-scatter.15
  378.7 21.2 reduce-scatter.17
  402.3 30.0 reduce-scatter.13
  434.6 30.0 reduce-scatter.19
  466.9 50.9 reduce-scatter.21
  520.2 51.7 reduce-scatter.23
  574.1 51.7 reduce-scatter.25
  629.1 53.8 all-reduce.29
  685.5 59.3 all-reduce.31
Sparse Core Ops, SparseCore 1:
  116.4 32.4 all-gather.3
  150.3 31.5 all-gather.5
  183.2 31.5 all-gather.7
